TPU v7x, 256 devices: a whole 4x4x8 slice. The times are simulated.
256 devices in a mesh: snap: 8 (over y, core), vtx: 32 (over z, x).
Axes of the slice: x: 4, y: 4, z: 8, core: 2. Of those that a mesh axis runs over, the one named last changes fastest.
Arguments:
- features: bfloat16 [16, 32768, 128], P('snap', 'vtx'), may hold values from -6 to 6
- tile_vals: bfloat16 [16, 256, 16, 128, 128], P('snap', 'vtx'), may hold values from -0.25 to 0.25
- tile_cols: int32 [16, 256, 16], P('snap', 'vtx'), may hold values from 0 to 255, as said below
- tile_count: int32 [16, 256], P('snap', 'vtx'), may hold values from 1 to 16
- gcn_weight: bfloat16 [128, 128], replicated, may hold values from -0.5 to 0.5
- gcn_bias: float32 [128], replicated, may hold values from -3 to 3
- input_weight: bfloat16 [128, 512], replicated, may hold values from -0.5 to 0.5
- recur_weight: bfloat16 [128, 512], replicated, may hold values from -0.5 to 0.5
- lstm_bias: float32 [512], replicated, may hold values from -4 to 4
- hidden_grad: bfloat16 [32, 1024, 16, 128], P('vtx', 'snap'), may hold values from -6 to 6
Outputs:
- hidden_states: bfloat16 [32, 1024, 16, 128], P('vtx', 'snap')
- grad_gcn_weight: float32 [128, 128], replicated
- grad_gcn_bias: float32 [128], replicated
- grad_input_weight: float32 [128, 512], replicated
- grad_recur_weight: float32 [128, 512], replicated
- grad_lstm_bias: float32 [512], replicated
Inputs may be any that keep to these rules, and one draw needn't show every extreme that they name: `tile_cols`: within one snapshot, the 16 slots of one row block name distinct column blocks, and all slots, live or not, of the row blocks j * 8 to (j + 1) * 8 - 1 together name at most one block of each group of 8 consecutive blocks.
All inputs are finite; a program needn't handle non-finite values.
Results may differ from a plain program's by a relative error of at most 0.0085.
Values may be sent and summed in bfloat16 or wider, within the bound.
No kernel may reach another device: no remote copies, remote signals or barrier semaphores. Data moves between devices by JAX's collectives and lax.ppermute only.
A program may use at most 128 MiB of HBM per device.

v0:
```python
import jax
import jax.numpy as jnp
from jax import lax
from jax.sharding import PartitionSpec as P


def silu_slope(grad_layer, pre_act):
    squeeze = jax.nn.sigmoid(pre_act)
    return (grad_layer.astype(jnp.float32) * squeeze * (1.0 + pre_act * (1.0 - squeeze))).astype(
        jnp.bfloat16
    )


def on_device(
    features,
    tile_vals,
    tile_cols,
    tile_count,
    gcn_weight,
    gcn_bias,
    input_weight,
    recur_weight,
    lstm_bias,
    hidden_grad,
):
    steps_dev, local_verts, feat_width = features.shape
    tile_size = tile_vals.shape[3]
    hidden_size = recur_weight.shape[0]
    live_mask = lax.broadcasted_iota(jnp.int32, tile_cols.shape, 2) < tile_count[:, :, None]
    snap_iota = lax.broadcasted_iota(jnp.int32, tile_cols.shape, 0)
    gathered = lax.all_gather(features, "vtx", axis=1, tiled=True)
    whole_blocks = gathered.reshape(steps_dev, -1, tile_size, feat_width)
    fetched_blocks = whole_blocks[snap_iota, tile_cols]
    blocks_used = jnp.where(
        live_mask[..., None, None], fetched_blocks, jnp.zeros_like(fetched_blocks)
    )
    summed = jnp.einsum(
        "svmij,svmjf->svif", tile_vals, blocks_used, preferred_element_type=jnp.float32
    )
    aggregated = summed.astype(jnp.bfloat16).reshape(steps_dev * local_verts, feat_width)
    pre_act = jnp.dot(aggregated, gcn_weight, preferred_element_type=jnp.float32) + gcn_bias
    layer_out = (
        jax.nn.silu(pre_act).astype(jnp.bfloat16).reshape(steps_dev, local_verts, feat_width)
    )
    vertex_inputs = lax.all_to_all(layer_out, "snap", split_axis=1, concat_axis=0, tiled=True)
    total_steps, vertex_rows, _ = vertex_inputs.shape
    flat_inputs = vertex_inputs.reshape(total_steps * vertex_rows, feat_width)
    input_gates = (
        jnp.dot(flat_inputs, input_weight, preferred_element_type=jnp.float32) + lstm_bias
    ).reshape(total_steps, vertex_rows, 4 * hidden_size)

    def advance(carried, gates_step):
        cell_state, last_out = carried
        pre_gates = gates_step + jnp.dot(last_out, recur_weight, preferred_element_type=jnp.float32)
        gate_in = jax.nn.sigmoid(pre_gates[:, :hidden_size])
        gate_keep = jax.nn.sigmoid(pre_gates[:, hidden_size : 2 * hidden_size])
        gate_new = jnp.tanh(pre_gates[:, 2 * hidden_size : 3 * hidden_size])
        gate_out = jax.nn.sigmoid(pre_gates[:, 3 * hidden_size :])
        cell_state = gate_keep * cell_state + gate_in * gate_new
        new_out = (gate_out * jnp.tanh(cell_state)).astype(jnp.bfloat16)
        return ((cell_state, new_out), (pre_gates, cell_state, new_out))

    zero_cell = jnp.zeros((vertex_rows, hidden_size), jnp.float32)
    start = (zero_cell, jnp.zeros((vertex_rows, hidden_size), jnp.bfloat16))
    _, (all_pre, all_cells, all_outs) = lax.scan(advance, start, input_gates)
    prev_cells = jnp.concatenate([zero_cell[None], all_cells[:-1]], axis=0)
    prev_outs = jnp.concatenate([start[1][None], all_outs[:-1]], axis=0)
    grad_outs = jnp.transpose(hidden_grad[0], (1, 0, 2)).astype(jnp.float32)

    def retreat(carried, step_items):
        grad_cell, grad_back = carried
        pre_gates, cell_state, prev_cell, grad_out = step_items
        gate_in = jax.nn.sigmoid(pre_gates[:, :hidden_size])
        gate_keep = jax.nn.sigmoid(pre_gates[:, hidden_size : 2 * hidden_size])
        gate_new = jnp.tanh(pre_gates[:, 2 * hidden_size : 3 * hidden_size])
        gate_out = jax.nn.sigmoid(pre_gates[:, 3 * hidden_size :])
        squash = jnp.tanh(cell_state)
        grad_total = grad_out + grad_back
        grad_cell = grad_cell + grad_total * gate_out * (1.0 - squash * squash)
        grad_gates = jnp.concatenate(
            [
                grad_cell * gate_new * gate_in * (1.0 - gate_in),
                grad_cell * prev_cell * gate_keep * (1.0 - gate_keep),
                grad_cell * gate_in * (1.0 - gate_new * gate_new),
                grad_total * squash * gate_out * (1.0 - gate_out),
            ],
            axis=1,
        ).astype(jnp.bfloat16)
        grad_back = jnp.einsum(
            "rg,hg->rh", grad_gates, recur_weight, preferred_element_type=jnp.float32
        )
        return ((grad_cell * gate_keep, grad_back), grad_gates)

    _, all_grad_gates = lax.scan(
        retreat, (zero_cell, zero_cell), (all_pre, all_cells, prev_cells, grad_outs), reverse=True
    )
    flat_gates = all_grad_gates.reshape(total_steps * vertex_rows, 4 * hidden_size)
    grad_input = jnp.einsum(
        "rf,rg->fg", flat_inputs, flat_gates, preferred_element_type=jnp.float32
    )
    grad_recur = jnp.einsum(
        "rh,rg->hg",
        prev_outs.reshape(total_steps * vertex_rows, hidden_size),
        flat_gates,
        preferred_element_type=jnp.float32,
    )
    grad_bias = jnp.sum(flat_gates.astype(jnp.float32), axis=0)
    grad_layer = jnp.einsum(
        "rg,fg->rf", flat_gates, input_weight, preferred_element_type=jnp.float32
    ).astype(jnp.bfloat16)
    grad_snap = lax.all_to_all(
        grad_layer.reshape(total_steps, vertex_rows, feat_width),
        "snap",
        split_axis=0,
        concat_axis=1,
        tiled=True,
    )
    grad_snap = grad_snap.reshape(steps_dev * local_verts, feat_width)
    grad_pre = silu_slope(grad_snap, pre_act)
    grad_gcn = jnp.einsum("rf,rg->fg", aggregated, grad_pre, preferred_element_type=jnp.float32)
    grad_gbias = jnp.sum(grad_pre.astype(jnp.float32), axis=0)
    grad_gcn, grad_gbias, grad_input, grad_recur, grad_bias = lax.psum(
        (grad_gcn, grad_gbias, grad_input, grad_recur, grad_bias), ("snap", "vtx")
    )
    hidden_states = jnp.transpose(all_outs, (1, 0, 2))[None]
    return (hidden_states, grad_gcn, grad_gbias, grad_input, grad_recur, grad_bias)


def solution(mesh):
    return jax.shard_map(
        on_device,
        mesh=mesh,
        in_specs=(
            P("snap", "vtx", None),
            P("snap", "vtx", None, None, None),
            P("snap", "vtx", None),
            P("snap", "vtx"),
            P(),
            P(),
            P(),
            P(),
            P(),
            P("vtx", "snap", None, None),
        ),
        out_specs=(P("vtx", "snap", None, None), P(), P(), P(), P(), P()),
        check_vma=False,
    )
```

profile of v0, /device:TPU:1, one launch (start us, length us, event | category | flops | bytes accessed | tf_op | source)
XLA Modules:
  0.0 570.2 jit_solution(6579747021246747212)
XLA Ops:
  9.5 145.1 %all-gather.2.cloned.1.call-done = bf16[2,32768,128]{2,1,0:T(8,128)(2,1)} async-done(((bf16[2,1024,128]{2,1,0:T(8,128)(2,1)}), bf16[2,32768,128]{2,1,0:T(8,128)(2,1)}) %all-gather.2.cloned.1.call-update) | async-done | bytes 16777232 | tf_op jit(solution)/shard_map/all_gather | solution.py:31
  154.6 15.9 %gather_fusion = bf16[256,128,128]{2,1,0:T(8,128)(2,1)} fusion(bf16[2,256,128,128]{3,2,1,0:T(8,128)(2,1)} %bitcast.136, s32[256]{0:T(256)S(1)} %reshape.144), kind=kCustom, calls=%fused_computation | custom fusion | bytes 16779264 | tf_op jit(solution)/shard_map/gather | solution.py:33
  170.4 8.2 %fusion.53 = bf16[2,8,128,128]{2,3,1,0:T(8,128)(2,1)S(1)} fusion(bf16[2,8,16,128,128]{4,3,2,1,0:T(8,128)(2,1)} %param.15, bf16[2,8,16,128,128]{4,3,2,1,0:T(8,128)(2,1)} %bitcast.132, pred[2,8,16]{2,1,0:T(8,128)(4,1)S(1)} %iota_compare_fusion), kind=kOutput, calls=%fused_computation.77 | convolution fusion | flops 1078198272 | bytes 17301760 | tf_op jit(solution)/shard_map/svmij,svmjf->svif/dot_general | solution.py:37
  182.2 5.3 all-to-all-start
  188.6 8.3 %all-to-all-done = bf16[2,1024,128]{2,0,1:T(2,128)(2,1)S(1)} async-done(((bf16[2,1024,128]{2,0,1:T(2,128)(2,1)}), bf16[2,1024,128]{2,0,1:T(2,128)(2,1)S(1)}, u32[]{:S(2)}, u32[]{:S(2)}) %all-to-all-start) | async-done | bytes 524320 | tf_op jit(solution)/shard_map/all_to_all | solution.py:45
  197.1 2.6 convolution_add_fusion.1
  199.7 41.2 %while.38 = (s32[]{:T(128)}, f32[128,128]{1,0:T(8,128)S(1)}, bf16[128,128]{1,0:T(8,128)(2,1)S(1)}, f32[16,128,512]{2,1,0:T(8,128)}, f32[16,128,128]{2,1,0:T(8,12...) while((s32[]{:T(128)}, f32[128,128]{1,0:T(8,128)S(1)}, ...), condition=%wide.region_1.2_spmd.clone, body=%wide.region_0.1_spmd.clone.sunk | while | flops 17104900 | bytes 1541236 | solution.py:65
  199.7 1.9 bitcast_dynamic-update-slice_fusion.6
  202.3 1.8 bitcast_dynamic-update-slice_fusion.6
  204.9 1.9 bitcast_dynamic-update-slice_fusion.6
  210.0 1.8 bitcast_dynamic-update-slice_fusion.6
  220.3 1.9 bitcast_dynamic-update-slice_fusion.6
  225.5 1.8 bitcast_dynamic-update-slice_fusion.6
  228.0 1.8 bitcast_dynamic-update-slice_fusion.6
  233.2 1.8 bitcast_dynamic-update-slice_fusion.6
  235.7 1.9 bitcast_dynamic-update-slice_fusion.6
  238.3 1.9 bitcast_dynamic-update-slice_fusion.6
  242.5 49.4 %while.39 = (s32[]{:T(128)}, f32[128,128]{1,0:T(8,128)S(1)}, f32[128,128]{1,0:T(8,128)S(1)}, bf16[16,128,512]{2,1,0:T(8,128)(2,1)S(1)}, f32[16,128,128]{2,1,0:T(...) while((s32[]{:T(128)}, f32[128,128]{1,0:T(8,128)S(1)}, ...), condition=%wide.region_3.4_spmd.clone, body=%wide.region_2.3_spmd.clone.sunk | while | flops 18481156 | bytes 2162843 | solution.py:94
  291.9 2.1 copy.34
  295.5 4.3 all-to-all-start.1
  299.8 2.2 convolution_bitcast_fusion
  303.1 6.1 %all-to-all-done.1 = bf16[16,128,128]{2,1,0:T(8,128)(2,1)S(1)} async-done(((bf16[16,128,128]{2,1,0:T(8,128)(2,1)}), bf16[16,128,128]{2,1,0:T(8,128)(2,1)S(1)}, u32[]{:S(2)}, u32[]{:S(2)}) %all-to-all-start.1) | async-done | bytes 524320 | tf_op jit(solution)/shard_map/all_to_all | solution.py:111
  313.4 73.9 %all-reduce.2 = (f32[128]{0:T(128)}, f32[512]{0:T(512)}) all-reduce(f32[128]{0:T(128)S(1)} %get-tuple-element.334, f32[512]{0:T(512)S(1)} %convert_reduce_fusion), channel_id=1, replica_groups=mesh['snap'=8,'vtx'=32] {'snap','vtx'}, use_global_device_ids=true, to_apply=%region_6.7 | all-reduce | flops 640 | bytes 5120 | tf_op jit(solution)/shard_map/psum | solution.py:122
  387.4 171.2 %all-reduce.6.cloned.1.call-done = (f32[128,128]{1,0:T(8,128)}, f32[128,512]{1,0:T(8,128)}, f32[128,512]{1,0:T(8,128)}) async-done(((f32[128,128]{1,0:T(8,128)}, f32[128,512]{1,0:T(8,128)}, f32[128,512]{1,0:T(8,128)}), (f32[128,128]{1,0:T(8,128)}, f32[128,512]{1,0:T(8,128)}, f32[128,512]{1,0:T(8,128)})) %all-reduce.6.cloned.1.call-update) | async-done | bytes 589840 | tf_op jit(solution)/shard_map/psum | solution.py:122
  (173 shorter events, 91.3 us)
Async XLA Ops:
  7.2 189.9 %copy-start = (bf16[128,512]{1,0:T(8,128)(2,1)S(1)}, bf16[128,512]{1,0:T(8,128)(2,1)}, u32[]{:S(2)}) copy-start(bf16[128,512]{1,0:T(8,128)(2,1)} %param.20) | copy-start | bytes 393220
  7.2 147.4 %all-gather.2.cloned.1.call-start = ((), (), s32[]{:S(2)}) async-start(), calls=%async_computation.2 | async-start | bytes 17301504 | tf_op jit(solution)/shard_map/all_gather | solution.py:31
  170.4 9.0 %copy-start.9 = (bf16[128,128]{1,0:T(8,128)(2,1)S(1)}, bf16[128,128]{1,0:T(8,128)(2,1)}, u32[]{:S(2)}) copy-start(bf16[128,128]{1,0:T(8,128)(2,1)} %param.18) | copy-start | bytes 98308
  170.4 9.0 %copy-start.10 = (f32[128]{0:T(128)S(1)}, f32[128]{0:T(128)}, u32[]{:S(2)}) copy-start(f32[128]{0:T(128)} %param.19) | copy-start | bytes 1540
  178.6 0.8 copy-start.6
  178.6 8.9 %copy-start.5 = (bf16[1,128,16,128]{3,2,1,0:T(8,128)(2,1)S(1)}, bf16[1,128,16,128]{3,2,1,0:T(8,128)(2,1)}, u32[]{:S(2)}) copy-start(bf16[1,128,16,128]{3,2,1,0:T(8,128)(2,1)} %param.23) | copy-start | bytes 1572868
  180.8 16.3 %copy-start.8 = (f32[512]{0:T(512)S(1)}, f32[512]{0:T(512)}, u32[]{:S(2)}) copy-start(f32[512]{0:T(512)} %param.22) | copy-start | bytes 6148
  182.2 14.8 %all-to-all-start = ((bf16[2,1024,128]{2,0,1:T(2,128)(2,1)}), bf16[2,1024,128]{2,0,1:T(2,128)(2,1)S(1)}, u32[]{:S(2)}, u32[]{:S(2)}) async-start(bf16[2,1024,128]{2,0,1:T(2,128)(2,1)} %copy.28), calls=%async_computation | async-start | bytes 1048576 | tf_op jit(solution)/shard_map/all_to_all | solution.py:45
  187.5 12.2 %copy-start.1 = (bf16[128,512]{1,0:T(8,128)(2,1)S(1)}, bf16[128,512]{1,0:T(8,128)(2,1)}, u32[]{:S(2)}) copy-start(bf16[128,512]{1,0:T(8,128)(2,1)} %param.21) | copy-start | bytes 393220
  240.9 1.3 copy-start.3
  295.5 13.8 %all-to-all-start.1 = ((bf16[16,128,128]{2,1,0:T(8,128)(2,1)}), bf16[16,128,128]{2,1,0:T(8,128)(2,1)S(1)}, u32[]{:S(2)}, u32[]{:S(2)}) async-start(bf16[16,128,128]{2,1,0:T(8,128)(2,1)} %bitcast.143), calls=%async_computation.1 | async-start | bytes 1048576 | tf_op jit(solution)/shard_map/all_to_all | solution.py:111
  299.8 258.8 %all-reduce.6.cloned.1.call-start = ((), (), s32[]{:S(2)}) async-start(), calls=%async_computation.3 | async-start | bytes 1179648 | tf_op jit(solution)/shard_map/psum | solution.py:122
  303.1 8.8 %copy-start.2 = (bf16[16,128,128]{2,1,0:T(8,128)(2,1)S(1)}, bf16[16,128,128]{2,1,0:T(8,128)(2,1)}, u32[]{:S(2)}) copy-start(bf16[16,128,128]{2,1,0:T(8,128)(2,1)} %get-tuple-element.229) | copy-start | bytes 1572868
  309.3 1.2 copy-start.4
  309.3 1.7 copy-start.7
Sparse Core Ops, SparseCore 0:
  10.6 143.9 all-gather.1
  312.1 246.4 all-reduce.5
where the time goes:
time: 573 us; the launch traced here: 570 us
  waiting for transfers between devices  331 us (58%)
  blocking collectives  73.9 us (13%)
  matrix products  50.5 us (9%)
  other arithmetic  44.9 us (8%)
  local copies, waits for them, and re-layouts  44.5 us (8%)
  between operations  14.2 us (2%)
  starting transfers between devices  9.64 us (2%)
    psum x1, waiting for transfers between devices, on_device(): lax.psum((grad_gcn, grad_gbias, grad_input, grad_recur, grad_bias), ('sna...  171 us
    all_gather x1, waiting for transfers between devices, on_device(): gathered = lax.all_gather(features, 'vtx', axis=1, tiled=True)  145 us
    psum x1, blocking collectives, on_device(): lax.psum((grad_gcn, grad_gbias, grad_input, grad_recur, grad_bias), ('sna...  73.9 us
    another operation x32, other arithmetic  29.8 us
    dot_general x16, matrix products, advance(): jnp.dot(last_out, recur_weight, preferred_element_type=jnp.float32)  29.5 us
    gather x1, local copies, waits for them, and re-layouts, on_device(): fetched_blocks = whole_blocks[snap_iota, tile_cols]  15.9 us
    squeeze x16, local copies, waits for them, and re-layouts, on_device(): _, (all_pre, all_cells, all_outs) = lax.scan(advance, start, input_gates)  15.6 us
  transfers between devices with their start and end apart: 4, of which 4 were waited for; matrix products, arithmetic and copies ran while one was open for 1% of the time, Pallas kernels for 0%

commit v1 on v0

--- a/solution.py
+++ b/solution.py
@@ -2,6 +2,14 @@
 import jax.numpy as jnp
 from jax import lax
 from jax.sharding import PartitionSpec as P
+from jax.lax import all_to_all, axis_size
+
+
+def return_all_pages(xin):
+    o_now = jnp.stack([xin] * axis_size("vtx"), 0)
+    local_part = all_to_all(o_now, axis_name="vtx", split_axis=0, concat_axis=0)
+    lower = jnp.concatenate(local_part, 1)
+    return lower
 
 
 def silu_slope(grad_layer, pre_act):
@@ -28,7 +36,7 @@
     hidden_size = recur_weight.shape[0]
     live_mask = lax.broadcasted_iota(jnp.int32, tile_cols.shape, 2) < tile_count[:, :, None]
     snap_iota = lax.broadcasted_iota(jnp.int32, tile_cols.shape, 0)
-    gathered = lax.all_gather(features, "vtx", axis=1, tiled=True)
+    gathered = return_all_pages(features)
     whole_blocks = gathered.reshape(steps_dev, -1, tile_size, feat_width)
     fetched_blocks = whole_blocks[snap_iota, tile_cols]
     blocks_used = jnp.where(

time: 573 us -> 856 us (1.49)
  waiting for transfers between devices: 331 us -> 569 us
  local copies, waits for them, and re-layouts: 44.5 us -> 65.4 us
  blocking collectives: 73.9 us -> 87.5 us
  starting transfers between devices: 9.64 us -> 22.3 us
    all_to_all x0 -> x1, waiting for transfers between devices: none -> 383 us  [return_all_pages(): local_part = all_to_all(o_now, axis_name='vtx', split_axis=0, concat_axis=0)]
    all_gather x1 -> x0, waiting for transfers between devices: 145 us -> none  [on_device(): gathered = lax.all_gather(features, 'vtx', axis=1, tiled=True)]
    all_to_all x0 -> x1, local copies, waits for them, and re-layouts: none -> 13.8 us  [return_all_pages(): local_part = all_to_all(o_now, axis_name='vtx', split_axis=0, concat_axis=0)]
    psum x1, blocking collectives: 73.9 us -> 87.5 us  [on_device(): lax.psum((grad_gcn, grad_gbias, grad_input, grad_recur, grad_bias), ('sna...]
    all_to_all x0 -> x1, starting transfers between devices: none -> 12.1 us  [return_all_pages(): local_part = all_to_all(o_now, axis_name='vtx', split_axis=0, concat_axis=0)]
where the time goes in v1:
time: 856 us; the launch traced here: 853 us
  waiting for transfers between devices  569 us (66%)
  blocking collectives  87.5 us (10%)
  local copies, waits for them, and re-layouts  65.4 us (8%)
  matrix products  50.4 us (6%)
  other arithmetic  43.6 us (5%)
  starting transfers between devices  22.3 us (3%)
  between operations  14.2 us (2%)
    all_to_all x1, waiting for transfers between devices, return_all_pages(): local_part = all_to_all(o_now, axis_name='vtx', split_axis=0, concat_axis=0)  383 us
    psum x1, waiting for transfers between devices, on_device(): lax.psum((grad_gcn, grad_gbias, grad_input, grad_recur, grad_bias), ('sna...  171 us
    psum x1, blocking collectives, on_device(): lax.psum((grad_gcn, grad_gbias, grad_input, grad_recur, grad_bias), ('sna...  87.5 us
    another operation x32, other arithmetic  29.8 us
    dot_general x16, matrix products, advance(): jnp.dot(last_out, recur_weight, preferred_element_type=jnp.float32)  29.4 us
  transfers between devices with their start and end apart: 4, of which 4 were waited for; matrix products, arithmetic and copies ran while one was open for 1% of the time, Pallas kernels for 0%

profile of v1, /device:TPU:1, one launch (start us, length us, event | category | flops | bytes accessed | tf_op | source)
XLA Modules:
  0.0 852.9 jit_solution(12356946114949138079)
XLA Ops:
  7.2 7.0 stack.2
  14.2 12.1 %all-to-all-start = ((bf16[32,2,1024,128]{3,2,1,0:T(8,128)(2,1)}), bf16[32,2,1024,128]{3,2,1,0:T(8,128)(2,1)}, u32[]{:S(2)}, u32[]{:S(2)}) async-start(bf16[32,2,1024,128]{3,2,1,0:T(8,128)(2,1)} %stack.2), calls=%async_computation | async-start | bytes 33554432 | tf_op jit(solution)/shard_map/all_to_all | solution.py:10
  26.5 382.9 %all-to-all-done = bf16[32,2,1024,128]{3,2,1,0:T(8,128)(2,1)} async-done(((bf16[32,2,1024,128]{3,2,1,0:T(8,128)(2,1)}), bf16[32,2,1024,128]{3,2,1,0:T(8,128)(2,1)}, u32[]{:S(2)}, u32[]{:S(2)}) %all-to-all-start) | async-done | bytes 16777248 | tf_op jit(solution)/shard_map/all_to_all | solution.py:10
  409.4 13.8 %copy.28 = bf16[32,2,1024,128]{3,2,0,1:T(8,128)(2,1)} copy(bf16[32,2,1024,128]{3,2,1,0:T(8,128)(2,1)} %all-to-all-done) | data formatting | bytes 33554432 | tf_op jit(solution)/shard_map/all_to_all | solution.py:10
  423.2 15.9 %gather_fusion = bf16[256,128,128]{2,1,0:T(8,128)(2,1)} fusion(bf16[2,256,128,128]{3,2,1,0:T(8,128)(2,1)} %bitcast.134, s32[256]{0:T(256)S(1)} %reshape.146), kind=kCustom, calls=%fused_computation | custom fusion | bytes 16779264 | tf_op jit(solution)/shard_map/gather | solution.py:41
  439.1 8.2 fusion.53
  450.9 5.9 all-to-all-start.1
  457.9 8.3 all-to-all-done.1
  466.4 2.6 convolution_add_fusion.1
  469.0 41.1 %while.38 = (s32[]{:T(128)}, f32[128,128]{1,0:T(8,128)S(1)}, bf16[128,128]{1,0:T(8,128)(2,1)S(1)}, f32[16,128,512]{2,1,0:T(8,128)}, f32[16,128,128]{2,1,0:T(8,12...) while((s32[]{:T(128)}, f32[128,128]{1,0:T(8,128)S(1)}, ...), condition=%wide.region_1.2_spmd.clone, body=%wide.region_0.1_spmd.clone.sunk | while | flops 17104900 | bytes 1541236 | solution.py:73
  469.0 1.8 bitcast_dynamic-update-slice_fusion.6
  471.6 1.8 bitcast_dynamic-update-slice_fusion.6
  474.2 1.8 bitcast_dynamic-update-slice_fusion.6
  489.5 1.8 bitcast_dynamic-update-slice_fusion.6
  494.7 1.8 bitcast_dynamic-update-slice_fusion.6
  504.9 1.9 bitcast_dynamic-update-slice_fusion.6
  507.5 1.9 bitcast_dynamic-update-slice_fusion.6
  511.6 49.4 %while.39 = (s32[]{:T(128)}, f32[128,128]{1,0:T(8,128)S(1)}, f32[128,128]{1,0:T(8,128)S(1)}, bf16[16,128,512]{2,1,0:T(8,128)(2,1)S(1)}, f32[16,128,128]{2,1,0:T(...) while((s32[]{:T(128)}, f32[128,128]{1,0:T(8,128)S(1)}, ...), condition=%wide.region_3.4_spmd.clone, body=%wide.region_2.3_spmd.clone.sunk | while | flops 18481156 | bytes 2162843 | solution.py:102
  561.1 2.1 copy.35
  564.7 4.3 all-to-all-start.2
  568.9 2.2 convolution_bitcast_fusion
  572.3 6.1 all-to-all-done.2
  582.6 87.5 %all-reduce.2 = (f32[128]{0:T(128)}, f32[512]{0:T(512)}) all-reduce(f32[128]{0:T(128)S(1)} %get-tuple-element.334, f32[512]{0:T(512)S(1)} %convert_reduce_fusion), channel_id=1, replica_groups=mesh['snap'=8,'vtx'=32] {'snap','vtx'}, use_global_device_ids=true, to_apply=%region_6.7 | all-reduce | flops 640 | bytes 5120 | tf_op jit(solution)/shard_map/psum | solution.py:130
  670.1 171.2 %all-reduce.6.cloned.1.call-done = (f32[128,128]{1,0:T(8,128)}, f32[128,512]{1,0:T(8,128)}, f32[128,512]{1,0:T(8,128)}) async-done(((f32[128,128]{1,0:T(8,128)}, f32[128,512]{1,0:T(8,128)}, f32[128,512]{1,0:T(8,128)}), (f32[128,128]{1,0:T(8,128)}, f32[128,512]{1,0:T(8,128)}, f32[128,512]{1,0:T(8,128)})) %all-reduce.6.cloned.1.call-update) | async-done | bytes 589840 | tf_op jit(solution)/shard_map/psum | solution.py:130
  (178 shorter events, 94.7 us)
Async XLA Ops:
  7.2 459.2 %copy-start = (bf16[128,512]{1,0:T(8,128)(2,1)S(1)}, bf16[128,512]{1,0:T(8,128)(2,1)}, u32[]{:S(2)}) copy-start(bf16[128,512]{1,0:T(8,128)(2,1)} %param.20) | copy-start | bytes 393220
  14.2 12.1 %copy-start.8 = (s32[2,8,16]{2,1,0:T(8,128)S(1)}, s32[2,8,16]{2,1,0:T(8,128)}, u32[]{:S(2)}) copy-start(s32[2,8,16]{2,1,0:T(8,128)} %param.16) | copy-start | bytes 3076
  14.2 12.2 %copy-start.10 = (s32[2,8]{1,0:T(2,128)S(1)}, s32[2,8]{1,0:T(2,128)}, u32[]{:S(2)}) copy-start(s32[2,8]{1,0:T(2,128)} %param.17) | copy-start | bytes 196
  14.2 395.2 %all-to-all-start = ((bf16[32,2,1024,128]{3,2,1,0:T(8,128)(2,1)}), bf16[32,2,1024,128]{3,2,1,0:T(8,128)(2,1)}, u32[]{:S(2)}, u32[]{:S(2)}) async-start(bf16[32,2,1024,128]{3,2,1,0:T(8,128)(2,1)} %stack.2), calls=%async_computation | async-start | bytes 33554432 | tf_op jit(solution)/shard_map/all_to_all | solution.py:10
  439.1 9.0 %copy-start.11 = (bf16[128,128]{1,0:T(8,128)(2,1)S(1)}, bf16[128,128]{1,0:T(8,128)(2,1)}, u32[]{:S(2)}) copy-start(bf16[128,128]{1,0:T(8,128)(2,1)} %param.18) | copy-start | bytes 98308
  439.1 9.0 %copy-start.12 = (f32[128]{0:T(128)S(1)}, f32[128]{0:T(128)}, u32[]{:S(2)}) copy-start(f32[128]{0:T(128)} %param.19) | copy-start | bytes 1540
  447.3 0.8 copy-start.6
  447.3 9.5 %copy-start.5 = (bf16[1,128,16,128]{3,2,1,0:T(8,128)(2,1)S(1)}, bf16[1,128,16,128]{3,2,1,0:T(8,128)(2,1)}, u32[]{:S(2)}) copy-start(bf16[1,128,16,128]{3,2,1,0:T(8,128)(2,1)} %param.23) | copy-start | bytes 1572868
  449.5 16.9 %copy-start.9 = (f32[512]{0:T(512)S(1)}, f32[512]{0:T(512)}, u32[]{:S(2)}) copy-start(f32[512]{0:T(512)} %param.22) | copy-start | bytes 6148
  450.9 15.4 %all-to-all-start.1 = ((bf16[2,1024,128]{2,0,1:T(2,128)(2,1)}), bf16[2,1024,128]{2,0,1:T(2,128)(2,1)S(1)}, u32[]{:S(2)}, u32[]{:S(2)}) async-start(bf16[2,1024,128]{2,0,1:T(2,128)(2,1)} %copy.29), calls=%async_computation.1 | async-start | bytes 1048576 | tf_op jit(solution)/shard_map/all_to_all | solution.py:53
  456.8 12.2 %copy-start.1 = (bf16[128,512]{1,0:T(8,128)(2,1)S(1)}, bf16[128,512]{1,0:T(8,128)(2,1)}, u32[]{:S(2)}) copy-start(bf16[128,512]{1,0:T(8,128)(2,1)} %param.21) | copy-start | bytes 393220
  510.1 1.3 copy-start.3
  564.7 13.8 %all-to-all-start.2 = ((bf16[16,128,128]{2,1,0:T(8,128)(2,1)}), bf16[16,128,128]{2,1,0:T(8,128)(2,1)S(1)}, u32[]{:S(2)}, u32[]{:S(2)}) async-start(bf16[16,128,128]{2,1,0:T(8,128)(2,1)} %bitcast.145), calls=%async_computation.2 | async-start | bytes 1048576 | tf_op jit(solution)/shard_map/all_to_all | solution.py:119
  568.9 272.3 %all-reduce.6.cloned.1.call-start = ((), (), s32[]{:S(2)}) async-start(), calls=%async_computation.3 | async-start | bytes 1179648 | tf_op jit(solution)/shard_map/psum | solution.py:130
  572.3 8.8 %copy-start.2 = (bf16[16,128,128]{2,1,0:T(8,128)(2,1)S(1)}, bf16[16,128,128]{2,1,0:T(8,128)(2,1)}, u32[]{:S(2)}) copy-start(bf16[16,128,128]{2,1,0:T(8,128)(2,1)} %get-tuple-element.229) | copy-start | bytes 1572868
  578.4 1.2 copy-start.4
  578.4 1.7 copy-start.7
Sparse Core Ops, SparseCore 0:
  581.2 260.0 all-reduce.5
